TPU v7x, 32 devices: a whole 2x2x4 slice. The times are simulated.
32 devices in a mesh: wide: 16 (over z, y, x), narrow: 2 (over core).
Axes of the slice: x: 2, y: 2, z: 4, core: 2. Of those that a mesh axis runs over, the one named last changes fastest.
Arguments:
- blocks: float32 [256, 14, 128, 128], P('wide', 'narrow'), may hold values from -0.125 to 0.125
- vectors: float32 [32768, 512], P('wide'), may hold values from -1.5 to 1.5
- sign_bits: int32 [32768], P('wide'), may hold values from 0 to 1
- column_blocks: int32 [256, 14], P('wide', 'narrow'), may hold values from 0 to 255, as said below
- sample_rows: int32 [1024], P('wide'), may hold values from 0 to 32767, as said below
Outputs:
- sketch: float32 [1024, 512], P('wide', 'narrow')
Inputs may be any that keep to these rules, and one draw needn't show every extreme that they name: `column_blocks`: entry [g, j] equals (g + o) mod 256 for an offset o with -8 <= o <= 8; both offsets -8 and 8 occur in every draw. `sample_rows`: entries 64 * w to 64 * w + 63 are distinct rows of slab w, that is of rows 16 * 128 * w to 16 * 128 * w + 16 * 128 - 1, in increasing order.
All inputs are finite; a program needn't handle non-finite values.
Results may differ from a plain program's by a relative error of at most 0.00013.
Values sent between devices are 32-bit elements; how exact they have to be, the bound alone decides.
A program may use at most 192 MiB of HBM per device.

v0:
```python
import functools
import math

import jax
import jax.numpy as jnp
from jax import lax
from jax.experimental import pallas as pl
from jax.experimental.pallas import tpu as pltpu
from jax.sharding import PartitionSpec as P

REACH = 8
MESH = pl.DeviceIdType.MESH


def split_bf16(x):
    high = x.astype(jnp.bfloat16)
    return high, (x - high.astype(jnp.float32)).astype(jnp.bfloat16)


def add_pairs(first, last, b, r, slots, order, which, columns, blocks, high, low, shift, total):
    def block(at):
        which_at = which[b, at]
        found = blocks[0][r, which_at % slots]
        for share in range(1, len(blocks)):
            found = jnp.where(which_at // slots == share, blocks[share][r, which_at % slots], found)
        return found

    group = 4

    def several(i, carry):
        parts = []
        for at in range(0, group, 2):
            entries = [first + group * i + at + k for k in range(2)]
            found = [jnp.minimum(e, last - 1) for e in entries]
            a = jnp.concatenate(
                [block(f) * (e < last).astype(jnp.float32) for e, f in zip(entries, found)], axis=1
            )
            a_high, a_low = split_bf16(a)
            where = [shift(columns[b, f]) for f in found]
            v_high = jnp.concatenate([high[w] for w in where], axis=0)
            v_low = jnp.concatenate([low[w] for w in where], axis=0)
            both = jnp.dot(
                jnp.concatenate([a_high, a_low], axis=0), v_high, preferred_element_type=jnp.float32
            )
            small = jnp.dot(a_high, v_low, preferred_element_type=jnp.float32)
            parts.append(both[:order] + (both[order:] + small))
        total[...] += functools.reduce(jnp.add, parts)
        return carry
    lax.fori_loop(0, (last - first + group - 1) // group, several, 0)


def convert_rows(piece, start, order, high, low):
    def convert(i, carry):
        h, l = split_bf16(piece[pl.ds(pl.multiple_of(i * order, order), order), :])
        high[start + i] = h
        low[start + i] = l
        return carry
    lax.fori_loop(0, piece.shape[0] // order, convert, 0)


def inside_kernel(shares, slots, order, which, columns, near, place, *refs):
    blocks, (inside, out, high, low) = refs[:shares], refs[shares:]
    step_rows = blocks[0].shape[0]
    step = pl.program_id(0)

    @pl.when(step == 0)
    def _():
        convert_rows(inside, 0, order, high, low)
    out[...] = jnp.zeros_like(out)

    def row(r, carry):
        b = step * step_rows + r
        add_pairs(
            0, near[b], b, r, slots, order, which, columns, blocks, high, low,
            lambda c: c - REACH, out.at[pl.ds(pl.multiple_of(r * order, order), order), :]
        )
        return carry
    lax.fori_loop(0, step_rows, row, 0)


def sketch_kernel(shares, slots, order, which, columns, near, rows, row_signs, *refs):
    blocks = refs[:shares]
    before, after, product, signs, hadamard, out, high, low, total, mixed = refs[shares:]
    step_rows = blocks[0].shape[0]
    slab_rows = signs.shape[0]
    step = pl.program_id(0)

    @pl.when(step == 0)
    def _():
        convert_rows(before, 0, order, high, low)
        convert_rows(after, REACH, order, high, low)

    def row(r, carry):
        b = step * step_rows + r
        total[...] = product[pl.ds(pl.multiple_of(r * order, order), order), :]
        add_pairs(
            near[b], which.shape[1], b, r, slots, order, which, columns, blocks, high, low,
            lambda c: jnp.where(c < REACH, c, c - slab_rows), total
        )
        stacked = jnp.concatenate(split_bf16(total[...]), axis=0)
        mix = (hadamard[...] * (2 * signs[b] - 1).astype(jnp.float32)).astype(jnp.bfloat16)
        mixed[pl.ds(pl.multiple_of(b * order, order), order), :] = jnp.dot(
            jnp.concatenate([mix, mix], axis=1), stacked, preferred_element_type=jnp.float32
        )
        return carry
    lax.fori_loop(0, step_rows, row, 0)

    @pl.when(step == pl.num_programs(0) - 1)
    def _():
        per_slab = out.shape[0] // row_signs.shape[0]
        group = 8

        def pick(i, carry):
            first = i * group
            sign = row_signs[first // per_slab]
            picked = [mixed[pl.ds(rows[first + k], 1), :] for k in range(group)]
            out[pl.ds(pl.multiple_of(first, group), group), :] = jnp.concatenate(picked, axis=0) * sign
            return carry
        lax.fori_loop(0, out.shape[0] // group, pick, 0, unroll=4)


def scatter_kernel(scale, x, out, held, total, last, send_sem, recv_sem, send_last, recv_last):
    far_count, near_count = x.shape[:2]
    me = lax.axis_index("wide")
    far_me, near_me = me // near_count, me % near_count

    def near_copy(p):
        to = (near_me + p) % near_count
        return pltpu.make_async_remote_copy(
            src_ref=x.at[:, to],
            dst_ref=held.at[p],
            send_sem=send_sem.at[p],
            recv_sem=recv_sem.at[p],
            device_id={"wide": far_me * near_count + to},
            device_id_type=MESH,
        )

    def far_copy(p):
        to = (far_me + p) % far_count
        return pltpu.make_async_remote_copy(
            src_ref=total.at[to],
            dst_ref=last.at[p],
            send_sem=send_last.at[p],
            recv_sem=recv_last.at[p],
            device_id={"wide": to * near_count + near_me},
            device_id_type=MESH,
        )

    def begin(copy):
        def body(p, carry):
            copy(p).start()
            return carry
        return body

    def end_near(p, carry):
        near_copy(p).wait()
        total[...] += held[p]
        return carry

    def end_far(p, carry):
        far_copy(p).wait()
        out[...] += last[p]
        return carry
    lax.fori_loop(1, near_count, begin(near_copy), 0)
    total[...] = x[:, near_me]
    lax.fori_loop(1, near_count, end_near, 0)
    lax.fori_loop(1, far_count, begin(far_copy), 0)
    out[...] = total[far_me]
    lax.fori_loop(1, far_count, end_far, 0)
    out[...] = out[...] * scale


def parity_sign(bits):
    return (1 - 2 * (lax.population_count(bits) & 1)).astype(jnp.float32)


def local(blocks, vectors, sign_bits, column_blocks, sample_rows):
    slab_rows, slots, order = blocks.shape[:3]
    width = vectors.shape[1]
    wide_count = lax.axis_size("wide")
    shares = lax.axis_size("narrow")
    half = width // shares
    me = lax.axis_index("wide")
    total_blocks = slab_rows * wide_count
    slab_total = slab_rows * order
    samples_slab = sample_rows.shape[0]
    samples = samples_slab * wide_count

    def widen(gathered, reach):
        radix = min(4, wide_count // reach)
        parts = [gathered]
        for k in range(1, radix):
            pairs = [(i, i ^ (k * reach)) for i in range(wide_count)]
            parts.append(lax.ppermute(gathered, "wide", pairs))
        return jnp.concatenate(parts, axis=0), reach * radix
    gathered, reach = widen(sample_rows[None], 1)
    narrow_me = lax.axis_index("narrow")
    reach_rows = REACH * order
    up = [(i, (i + 1) % wide_count) for i in range(wide_count)]
    down = [(j, i) for i, j in up]
    last_rows = lax.dynamic_slice(
        vectors, (slab_total - reach_rows, narrow_me * half), (reach_rows, half)
    )
    first_rows = lax.dynamic_slice(vectors, (0, narrow_me * half), (reach_rows, half))
    before = lax.ppermute(last_rows, "wide", up)
    after = lax.ppermute(first_rows, "wide", down)

    local_columns = (column_blocks - me * slab_rows + REACH) % total_blocks
    all_blocks, all_columns = [blocks], [local_columns]
    for shift in range(1, shares):
        pairs = [(i, (i + shift) % shares) for i in range(shares)]
        all_blocks.append(lax.ppermute(blocks, "narrow", pairs))
        all_columns.append(lax.ppermute(local_columns, "narrow", pairs))
    columns = jnp.concatenate(all_columns, axis=1)

    entries = shares * slots
    inside = ((columns >= REACH) & (columns < REACH + slab_rows)).astype(jnp.int32)
    places = jnp.arange(entries, dtype=jnp.int32)
    ahead = (places[None, :] < places[:, None]).astype(jnp.int32)[None]
    near = jnp.sum(inside, axis=1)
    rank = jnp.where(
        inside == 1,
        jnp.sum(inside[:, None, :] * ahead, axis=2),
        near[:, None] + jnp.sum((1 - inside)[:, None, :] * ahead, axis=2),
    )
    chosen = (rank[:, None, :] == places[None, :, None]).astype(jnp.int32)
    which = jnp.sum(chosen * places[None, None, :], axis=2)
    columns = jnp.sum(chosen * columns[:, None, :], axis=2)

    positions = jnp.arange(order, dtype=jnp.int32)
    hadamard = parity_sign(positions[:, None] & positions[None, :])

    def whole(shape):
        return pl.BlockSpec(shape, lambda b, *_: (0,) * len(shape), pipeline_mode=pl.Buffered(1))
    step_rows = math.gcd(slab_rows, 4)
    block_specs = [
        pl.BlockSpec((step_rows, slots, order, order), lambda b, *_: (b, 0, 0, 0))
        for _ in range(shares)
    ]
    row_spec = pl.BlockSpec((step_rows * order, half), lambda b, *_: (b, 0))
    flops = 2 * slab_rows * entries * order * order * half
    product = pl.pallas_call(
        functools.partial(inside_kernel, shares, slots, order),
        grid_spec=pltpu.PrefetchScalarGridSpec(
            num_scalar_prefetch=4,
            grid=(slab_rows // step_rows,),
            in_specs=block_specs + [
                pl.BlockSpec((slab_total, half), lambda b, *s: (0, s[3][0]), pipeline_mode=pl.Buffered(1))
            ],
            out_specs=row_spec,
            scratch_shapes=[pltpu.VMEM((slab_rows, order, half), jnp.bfloat16)] * 2,
        ),
        out_shape=jax.ShapeDtypeStruct((slab_total, half), jnp.float32),
        cost_estimate=pl.CostEstimate(flops=6 * flops, bytes_accessed=20 << 20, transcendentals=0),
        name="inside",
    )(which, columns, near, narrow_me.astype(jnp.int32).reshape(1), *all_blocks, vectors)
    gathered, product = lax.optimization_barrier((gathered, product))
    while reach < wide_count:
        gathered, reach = widen(gathered, reach)
    slabs = jnp.arange(wide_count, dtype=jnp.int32)
    rows = jnp.take(gathered, slabs ^ me, axis=0).reshape(samples) % slab_total
    row_signs = parity_sign(slabs & me)
    partial = pl.pallas_call(
        functools.partial(sketch_kernel, shares, slots, order),
        grid_spec=pltpu.PrefetchScalarGridSpec(
            num_scalar_prefetch=5,
            grid=(slab_rows // step_rows,),
            in_specs=block_specs + [
                whole((reach_rows, half)),
                whole((reach_rows, half)),
                row_spec,
                whole((slab_rows, 1, order)),
                whole((order, order)),
            ],
            out_specs=pl.BlockSpec((samples, half), lambda b, *_: (0, 0)),
            scratch_shapes=[
                pltpu.VMEM((2 * REACH, order, half), jnp.bfloat16),
                pltpu.VMEM((2 * REACH, order, half), jnp.bfloat16),
                pltpu.VMEM((order, half), jnp.float32),
                pltpu.VMEM((slab_total, half), jnp.float32),
            ],
        ),
        out_shape=jax.ShapeDtypeStruct((samples, half), jnp.float32),
        cost_estimate=pl.CostEstimate(flops=2 * flops, bytes_accessed=20 << 20, transcendentals=0),
        name="sketch",
    )(which, columns, near, rows, row_signs, *all_blocks, before, after, product,
      sign_bits.reshape(slab_rows, 1, order), hadamard)

    scale = math.sqrt(slab_total * wide_count / samples) / math.sqrt(order * wide_count)
    near_count = 1 << ((wide_count.bit_length() - 1) // 2)
    far_count = wide_count // near_count
    return pl.pallas_call(
        functools.partial(scatter_kernel, scale),
        in_specs=[pl.BlockSpec(memory_space=pltpu.VMEM)],
        out_specs=pl.BlockSpec(memory_space=pltpu.VMEM),
        out_shape=jax.ShapeDtypeStruct((samples_slab, half), jnp.float32),
        scratch_shapes=[
            pltpu.VMEM((near_count, far_count, samples_slab, half), jnp.float32),
            pltpu.VMEM((far_count, samples_slab, half), jnp.float32),
            pltpu.VMEM((far_count, samples_slab, half), jnp.float32),
            pltpu.SemaphoreType.DMA((near_count,)),
            pltpu.SemaphoreType.DMA((near_count,)),
            pltpu.SemaphoreType.DMA((far_count,)),
            pltpu.SemaphoreType.DMA((far_count,)),
        ],
        compiler_params=pltpu.CompilerParams(has_side_effects=True),
        name="scatter",
    )(partial.reshape(far_count, near_count, samples_slab, half))


def solution(mesh):
    return jax.shard_map(
        local,
        mesh=mesh,
        in_specs=(
            P("wide", "narrow", None, None),
            P("wide", None),
            P("wide"),
            P("wide", "narrow"),
            P("wide"),
        ),
        out_specs=P("wide", "narrow"),
        check_vma=False,
    )
```

profile of v0, /device:TPU:0, one launch (start us, length us, event | category | flops | bytes accessed | tf_op | source)
XLA Modules:
  0.0 105.7 jit_solution(265526799365850012)
XLA Ops:
  0.0 0.5 collective-permute-start.4
  0.5 3.5 %collective-permute-start.3 = (s32[1,64]{1,0:T(1,128)}, s32[1,64]{1,0:T(1,128)S(1)}, u32[]{:S(2)}, u32[]{:S(2)}) collective-permute-start(s32[1,64]{1,0:T(1,128)} %bitcast.8), channel_id=1, source_target_pairs={{0,6},{2,4},{4,2},{6,0},{8,14},{10,12},{12,10},{14,8},{16,22},{18,... | collective-permute-start | bytes 776 | tf_op jit(solution)/shard_map/ppermute | solution.py:194
  4.0 0.5 collective-permute-start.2
  4.5 0.1 collective-permute-start.1
  4.6 0.7 add_select_fusion.2
  5.4 0.6 subtract_convert_fusion.refs_6_
  6.0 1.7 %constant_dynamic-slice_fusion.1 = (f32[1024,256]{1,0:T(8,128)S(1)}, f32[1024,256]{1,0:T(8,128)S(1)}) fusion(f32[2048,512]{1,0:T(8,128)} %refs_2_.1, s32[]{:T(128)S(6)} %select_n.56), kind=kLoop, calls=%fused_computation.33 | loop fusion | bytes 4194308 | tf_op jit(solution)/shard_map/dynamic_slice | solution.py:204
  7.7 0.6 subtract_convert_fusion.1.row_signs
  8.3 5.9 %collective-permute-start.9 = (f32[1024,256]{1,0:T(8,128)S(1)}, f32[1024,256]{1,0:T(8,128)S(1)}, u32[]{:S(2)}, u32[]{:S(2)}) collective-permute-start(f32[1024,256]{1,0:T(8,128)S(1)} %get-tuple-element.15), channel_id=1, source_target_pairs={{2,0},{4,2},{6,4},{8,6},{10,8},{12,10},{14,12},{16,14},{18,16},{20... | collective-permute-start | bytes 3145736 | tf_op jit(solution)/shard_map/ppermute | solution.py:206
  14.5 0.5 multiply_reduce_fusion
  15.2 0.5 select_reduce_fusion
  15.7 0.7 copy.17.columns
  16.4 0.7 copy.16.which
  17.1 18.4 %inside.1.refs_4_ = f32[2048,256]{1,0:T(8,128)} custom-call(s32[16,14]{1,0:T(8,128)} %copy.16.which, s32[16,14]{1,0:T(8,128)} %copy.17.columns, s32[16]{0:T(128)} %copy-done.1, s32[1]{0:T(128)} %bitcast.1.place, f32[16,7,128,128]{3,2,1,0:T(8,128)} %refs_0_.3, f32[16,7,128,128]{3,2,1,0:T(8,128)} %collective-permute-done.4.refs_1_, f32[2048,512]{1,0:T(8,128)} %refs_2_.1), custom_call_target="tpu_custom_call" | custom-call | flops 11274289152 | bytes 20971520 | tf_op jit(solution)/shard_map/inside/pallas_call | solution.py:242
  35.5 3.4 %collective-permute-start.7 = (s32[4,64]{1,0:T(4,128)S(1)}, s32[4,64]{1,0:T(4,128)S(1)}, u32[]{:S(2)}, u32[]{:S(2)}) collective-permute-start(s32[4,64]{1,0:T(4,128)S(1)} %pad_add_fusion.2), channel_id=1, source_target_pairs={{0,24},{2,26},{4,28},{6,30},{8,16},{10,18},{12,20},{14,22},{16,8},... | collective-permute-start | bytes 3080 | tf_op jit(solution)/shard_map/ppermute | solution.py:194
  38.9 1.0 collective-permute-start.5
  39.9 1.0 collective-permute-done.7
  40.9 2.5 %collective-permute-done.6 = s32[4,64]{1,0:T(4,128)S(1)} collective-permute-done((s32[4,64]{1,0:T(4,128)S(1)}, s32[4,64]{1,0:T(4,128)S(1)}, u32[]{:S(2)}, u32[]{:S(2)}) %collective-permute-start.6) | collective-permute-done | bytes 1056 | tf_op jit(solution)/shard_map/ppermute | solution.py:194
  43.4 0.6 gather_fusion
  44.1 0.6 add_select_fusion.1.rows
  44.7 12.9 %collective-permute-done.8.refs_2_ = f32[1024,256]{1,0:T(8,128)} collective-permute-done((f32[1024,256]{1,0:T(8,128)S(1)}, f32[1024,256]{1,0:T(8,128)}, u32[]{:S(2)}, u32[]{:S(2)}) %collective-permute-start.8) | collective-permute-done | bytes 1048608 | tf_op jit(solution)/shard_map/ppermute | solution.py:205
  57.6 18.4 %sketch.1 = f32[1024,256]{1,0:T(8,128)} custom-call(s32[16,14]{1,0:T(8,128)} %copy.16.which, s32[16,14]{1,0:T(8,128)} %copy.17.columns, s32[16]{0:T(128)} %copy-done.1, s32[1024]{0:T(1024)} %add_select_fusion.1.rows, f32[16]{0:T(128)} %subtract_convert_fusion.1.row_signs, f32[16,7,128,128]{3,2,1,0:T(8,128)} %refs_0_.3, ...), custom_call_target="tpu_custom_call" | custom-call | flops 3758096384 | bytes 20971520 | tf_op jit(solution)/shard_map/sketch/pallas_call | solution.py:263
  76.0 28.2 %scatter.1 = f32[64,256]{1,0:T(8,128)} custom-call(f32[4,4,64,256]{3,2,1,0:T(8,128)} %bitcast.6), custom_call_target="tpu_custom_call" | custom-call | tf_op jit(solution)/shard_map/scatter/pallas_call | solution.py:292
  104.2 1.5 %copy.19 = f32[64,256]{1,0:T(8,128)} copy(f32[64,256]{1,0:T(8,128)} %scatter.1) | data formatting | bytes 131072
  (32 shorter events, 0.6 us)
Async XLA Ops:
  0.0 14.2 %copy-start.2 = (s32[64]{0:T(128)S(1)}, s32[64]{0:T(128)}, u32[]{:S(2)}) copy-start(s32[64]{0:T(128)} %param.9) | copy-start | bytes 772
  0.0 17.1 %collective-permute-start.4 = (f32[16,7,128,128]{3,2,1,0:T(8,128)}, f32[16,7,128,128]{3,2,1,0:T(8,128)}, u32[]{:S(2)}, u32[]{:S(2)}) collective-permute-start(f32[16,7,128,128]{3,2,1,0:T(8,128)} %refs_0_.3), channel_id=1, source_target_pairs={{0,1},{1,0},{2,3},{3,2},{4,5},{5,4},{6,7},{7,6},{8,9},{9,8},{10,11... | collective-permute-start | bytes 22020104 | tf_op jit(solution)/shard_map/ppermute | solution.py:212
  0.5 7.8 %collective-permute-start.3 = (s32[1,64]{1,0:T(1,128)}, s32[1,64]{1,0:T(1,128)S(1)}, u32[]{:S(2)}, u32[]{:S(2)}) collective-permute-start(s32[1,64]{1,0:T(1,128)} %bitcast.8), channel_id=1, source_target_pairs={{0,6},{2,4},{4,2},{6,0},{8,14},{10,12},{12,10},{14,8},{16,22},{18,... | collective-permute-start | bytes 776 | tf_op jit(solution)/shard_map/ppermute | solution.py:194
  4.0 10.2 %collective-permute-start.2 = (s32[1,64]{1,0:T(1,128)}, s32[1,64]{1,0:T(1,128)S(1)}, u32[]{:S(2)}, u32[]{:S(2)}) collective-permute-start(s32[1,64]{1,0:T(1,128)} %bitcast.9), channel_id=1, source_target_pairs={{0,4},{2,6},{4,0},{6,2},{8,12},{10,14},{12,8},{14,10},{16,20},{18,... | collective-permute-start | bytes 776 | tf_op jit(solution)/shard_map/ppermute | solution.py:194
  4.5 9.7 %collective-permute-start.1 = (s32[1,64]{1,0:T(1,128)}, s32[1,64]{1,0:T(1,128)S(1)}, u32[]{:S(2)}, u32[]{:S(2)}) collective-permute-start(s32[1,64]{1,0:T(1,128)} %bitcast.10), channel_id=1, source_target_pairs={{0,2},{2,0},{4,6},{6,4},{8,10},{10,8},{12,14},{14,12},{16,18},{18,... | collective-permute-start | bytes 776 | tf_op jit(solution)/shard_map/ppermute | solution.py:194
  5.3 8.9 %collective-permute-start = (s32[16,7]{0,1:T(8,128)S(1)}, s32[16,7]{0,1:T(8,128)S(1)}, u32[]{:S(2)}, u32[]{:S(2)}) collective-permute-start(s32[16,7]{0,1:T(8,128)S(1)} %add_select_fusion.2), channel_id=1, source_target_pairs={{0,1},{1,0},{2,3},{3,2},{4,5},{5,4},{6,7},{7,6},{8,9},{9,8},{10,11... | collective-permute-start | bytes 1352 | tf_op jit(solution)/shard_map/ppermute | solution.py:213
  8.3 36.4 %collective-permute-start.9 = (f32[1024,256]{1,0:T(8,128)S(1)}, f32[1024,256]{1,0:T(8,128)S(1)}, u32[]{:S(2)}, u32[]{:S(2)}) collective-permute-start(f32[1024,256]{1,0:T(8,128)S(1)} %get-tuple-element.15), channel_id=1, source_target_pairs={{2,0},{4,2},{6,4},{8,6},{10,8},{12,10},{14,12},{16,14},{18,16},{20... | collective-permute-start | bytes 3145736 | tf_op jit(solution)/shard_map/ppermute | solution.py:206
  14.2 43.4 %collective-permute-start.8 = (f32[1024,256]{1,0:T(8,128)S(1)}, f32[1024,256]{1,0:T(8,128)}, u32[]{:S(2)}, u32[]{:S(2)}) collective-permute-start(f32[1024,256]{1,0:T(8,128)S(1)} %get-tuple-element.16), channel_id=1, source_target_pairs={{0,2},{2,4},{4,6},{6,8},{8,10},{10,12},{12,14},{14,16},{16,18},{18... | collective-permute-start | bytes 3145736 | tf_op jit(solution)/shard_map/ppermute | solution.py:205
  14.3 2.8 %copy-start.1 = (s32[16]{0:T(128)}, s32[16]{0:T(128)S(1)}, u32[]{:S(2)}) copy-start(s32[16]{0:T(128)S(1)} %get-tuple-element.13.near) | copy-start | bytes 196
  35.5 5.4 %collective-permute-start.7 = (s32[4,64]{1,0:T(4,128)S(1)}, s32[4,64]{1,0:T(4,128)S(1)}, u32[]{:S(2)}, u32[]{:S(2)}) collective-permute-start(s32[4,64]{1,0:T(4,128)S(1)} %pad_add_fusion.2), channel_id=1, source_target_pairs={{0,24},{2,26},{4,28},{6,30},{8,16},{10,18},{12,20},{14,22},{16,8},... | collective-permute-start | bytes 3080 | tf_op jit(solution)/shard_map/ppermute | solution.py:194
  38.9 4.5 %collective-permute-start.6 = (s32[4,64]{1,0:T(4,128)S(1)}, s32[4,64]{1,0:T(4,128)S(1)}, u32[]{:S(2)}, u32[]{:S(2)}) collective-permute-start(s32[4,64]{1,0:T(4,128)S(1)} %pad_add_fusion.2), channel_id=1, source_target_pairs={{0,16},{2,18},{4,20},{6,22},{8,24},{10,26},{12,28},{14,30},{16,0},... | collective-permute-start | bytes 3080 | tf_op jit(solution)/shard_map/ppermute | solution.py:194
  38.9 4.5 %collective-permute-start.5 = (s32[4,64]{1,0:T(4,128)S(1)}, s32[4,64]{1,0:T(4,128)S(1)}, u32[]{:S(2)}, u32[]{:S(2)}) collective-permute-start(s32[4,64]{1,0:T(4,128)S(1)} %pad_add_fusion.2), channel_id=1, source_target_pairs={{0,8},{2,10},{4,12},{6,14},{8,0},{10,2},{12,4},{14,6},{16,24},{18,... | collective-permute-start | bytes 3080 | tf_op jit(solution)/shard_map/ppermute | solution.py:194
  44.7 12.9 %copy-start = (f32[1024,256]{1,0:T(8,128)}, f32[1024,256]{1,0:T(8,128)S(1)}, u32[]{:S(2)}) copy-start(f32[1024,256]{1,0:T(8,128)S(1)} %collective-permute-done.9.refs_3_) | copy-start | bytes 3145732
where the time goes:
time: 106 us
  Pallas kernels  65 us (61%)
  waiting for transfers between devices  16.4 us (15%)
  starting transfers between devices  14.9 us (14%)
  local copies, waits for them, and re-layouts  5.47 us (5%)
  other arithmetic  3.8 us (4%)
    pallas_call x1, Pallas kernels, local(): pl.pallas_call(functools.partial(scatter_kernel, scale), in_specs=[pl.Blo...  28.2 us
    pallas_call x1, Pallas kernels, local(): pl.pallas_call(functools.partial(sketch_kernel, shares, slots, order), gr...  18.4 us
    pallas_call x1, Pallas kernels, local(): pl.pallas_call(functools.partial(inside_kernel, shares, slots, order), gr...  18.4 us
    ppermute x1, waiting for transfers between devices, local(): before = lax.ppermute(last_rows, 'wide', up)  12.9 us
    ppermute x6, starting transfers between devices, widen(): parts.append(lax.ppermute(gathered, 'wide', pairs))  8.52 us
    ppermute x1, starting transfers between devices, local(): after = lax.ppermute(first_rows, 'wide', down)  5.88 us
    ppermute x6, waiting for transfers between devices, widen(): parts.append(lax.ppermute(gathered, 'wide', pairs))  3.51 us
  transfers between devices with their start and end apart: 10, of which 3 were waited for; matrix products, arithmetic and copies ran while one was open for 7% of the time, Pallas kernels for 17%

commit v1 on v0

v1 whole, which is shorter than its diff:
```python
import functools
import math

import jax
import jax.numpy as jnp
from jax import lax
from jax.experimental import pallas as pl
from jax.experimental.pallas import tpu as pltpu
from jax.sharding import PartitionSpec as P

REACH = 8
LANES = 128
MESH = pl.DeviceIdType.MESH


def split_bf16(x):
    high = x.astype(jnp.bfloat16)
    return high, (x - high.astype(jnp.float32)).astype(jnp.bfloat16)


def parity_sign(bits, width):
    shift = 1 << max(width - 1, 1).bit_length() >> 1
    while shift:
        bits = bits ^ (bits >> shift)
        shift //= 2
    return (1 - 2 * (bits & 1)).astype(jnp.float32)


def within(value, count):
    return value & (count - 1) if count & (count - 1) == 0 else lax.rem(value, count)


def dot(a, b):
    return jnp.dot(a, b, preferred_element_type=jnp.float32)


def sketch_kernel(
    scale, blocks, vectors, signs, columns, samples, out,
    held_blocks, own, high, low, halo, wide_halo, outside, band, mixed, column_land, column_scalar, row_land,
    row_scalar, partial, first, first_land, second, second_land, third_land,
    local_sem, block_send, block_recv, halo_send, halo_recv, column_send, column_recv, row_send, row_recv,
    y_send, y_recv, z_send, z_recv, x_send, x_recv,
):
    wide = lax.axis_size("wide")
    shares = lax.axis_size("narrow")
    me, part = lax.axis_index("wide"), lax.axis_index("narrow")
    slab_rows, slots, order = blocks.shape[:3]
    slab_total = slab_rows * order
    total_blocks = slab_rows * wide
    width = out.shape[1]
    chunks = width // LANES
    per_slab = out.shape[0]
    reach_rows = REACH * order
    half_rows = slab_rows // 2
    x_me, y_me, z_me = me % 2, me // 2 % 2, me // 4
    z_count = wide // 4

    barrier = pltpu.get_barrier_semaphore()

    def greet(p, carry):
        pl.semaphore_signal(barrier, 1, device_id={"wide": (me + p) % wide}, device_id_type=MESH)
        return carry
    lax.fori_loop(1, wide, greet, 0)
    for p in range(1, shares):
        pl.semaphore_signal(barrier, 1, device_id={"narrow": (part + p) % shares}, device_id_type=MESH)

    own_copy = pltpu.make_async_copy(
        vectors.at[:, pl.ds(pl.multiple_of(part * width, LANES), width)], own, local_sem.at[slab_rows]
    )
    own_copy.start()

    def block_copy(b):
        return pltpu.make_async_copy(blocks.at[b], held_blocks.at[0, b], local_sem.at[b])

    def begin_blocks(b, carry):
        block_copy(b).start()
        return carry
    lax.fori_loop(0, slab_rows, begin_blocks, 0)
    own_columns = pltpu.make_async_copy(columns, column_scalar.at[0], local_sem.at[slab_rows + 1])
    own_columns.start()
    own_samples = pltpu.make_async_copy(samples, row_scalar.at[me], local_sem.at[slab_rows + 2])
    own_samples.start()

    pl.semaphore_wait(barrier, wide - 1 + shares - 1)

    def partner(p):
        return {"narrow": (part + p) % shares}

    def column_copy(p):
        return pltpu.make_async_remote_copy(
            src_ref=columns, dst_ref=column_land.at[p], send_sem=column_send.at[p], recv_sem=column_recv.at[p],
            device_id=partner(p), device_id_type=MESH,
        )

    def row_copy(p):
        return pltpu.make_async_remote_copy(
            src_ref=samples, dst_ref=row_land.at[p], send_sem=row_send.at[p], recv_sem=row_recv.at[p],
            device_id={"wide": (me + p) % wide}, device_id_type=MESH,
        )

    def share_copy(p, b):
        return pltpu.make_async_remote_copy(
            src_ref=blocks.at[b], dst_ref=held_blocks.at[p, b],
            send_sem=block_send.at[p, b], recv_sem=block_recv.at[p, b],
            device_id=partner(p), device_id_type=MESH,
        )

    def halo_copy(q, side):
        start = slab_total - reach_rows if side == 0 else 0
        to = (me + 1) % wide if side == 0 else (me + wide - 1) % wide
        return pltpu.make_async_remote_copy(
            src_ref=vectors.at[pl.ds(start, reach_rows), pl.ds(pl.multiple_of(part * width + q * LANES, LANES), LANES)],
            dst_ref=halo.at[q, side], send_sem=halo_send.at[q, side], recv_sem=halo_recv.at[q, side],
            device_id={"wide": to}, device_id_type=MESH,
        )

    for p in range(1, shares):
        column_copy(p).start()

    def begin_rows(p, carry):
        row_copy(p).start()
        return carry
    lax.fori_loop(1, wide, begin_rows, 0)
    for q in range(chunks):
        for side in range(2):
            halo_copy(q, side).start()

    def begin_shares(b, carry):
        for p in range(1, shares):
            share_copy(p, b).start()
        return carry
    lax.fori_loop(0, slab_rows, begin_shares, 0)

    own_copy.wait()

    def convert(i, carry):
        h, l = split_bf16(own[pl.ds(pl.multiple_of(i * order, order), order), :])
        high[i] = h
        low[i] = l
        return carry
    lax.fori_loop(0, slab_rows, convert, 0)
    high[slab_rows] = jnp.zeros(high.shape[1:], high.dtype)
    low[slab_rows] = jnp.zeros(low.shape[1:], low.dtype)

    own_columns.wait()
    for p in range(1, shares):
        column_copy(p).wait()
        there = pltpu.make_async_copy(column_land.at[p], column_scalar.at[p], local_sem.at[slab_rows + 1])
        there.start()
        there.wait()

    at_row = lax.broadcasted_iota(jnp.int32, (order, order), 0)
    at_column = lax.broadcasted_iota(jnp.int32, (order, order), 1)
    hadamard = parity_sign(at_row & at_column, (order - 1).bit_length())
    entries = [(p, j) for p in range(shares) for j in range(slots)]

    def row(b, carry):
        block_copy(b).wait()
        for p in range(1, shares):
            share_copy(p, b).wait()
        place = []
        for p, j in entries:
            at = column_scalar[p, b, j] - me * slab_rows + REACH
            at = jnp.where(at < 0, at + total_blocks, at)
            place.append(jnp.where(at >= total_blocks, at - total_blocks, at))
        left, left_high, right_high, right_low = [], [], [], []
        for (p, j), at in zip(entries, place):
            a_high, a_low = split_bf16(held_blocks[p, b, j])
            inside = (at >= REACH) & (at < REACH + slab_rows)
            where = jnp.where(inside, at - REACH, slab_rows)
            left.append(jnp.concatenate([a_high, a_low], axis=0))
            left_high.append(a_high)
            right_high.append(high[where])
            right_low.append(low[where])
        both = dot(jnp.concatenate(left, axis=1), jnp.concatenate(right_high, axis=0))
        small = dot(jnp.concatenate(left_high, axis=1), jnp.concatenate(right_low, axis=0))
        product = both[:order] + (both[order:] + small)

        first_out = jnp.where(b < half_rows, 0, REACH + slab_rows)
        for h in range(REACH):
            piece = jnp.zeros((order, order), jnp.float32)
            for (p, j), at in zip(entries, place):
                piece = piece + held_blocks[p, b, j] * (at - first_out == h).astype(jnp.float32)
            outside[:, h * order:(h + 1) * order] = piece

        sign = (2 * signs[b] - 1).astype(jnp.float32)
        mix = (hadamard * sign).astype(jnp.bfloat16)
        mix = jnp.concatenate([mix, mix], axis=1)
        mixed_row = dot(mix, jnp.concatenate(split_bf16(product), axis=0))
        for q in range(chunks):
            mixed[q, pl.ds(pl.multiple_of(b * order, order), order), :] = mixed_row[:, q * LANES:(q + 1) * LANES]
        turned = dot(mix, jnp.concatenate(split_bf16(outside[...]), axis=0))
        t_high, t_low = split_bf16(turned)
        band[b, :order] = t_high
        band[b, order:] = t_low
        return carry
    lax.fori_loop(0, slab_rows, row, 0)

    own_samples.wait()

    def end_rows(p, carry):
        row_copy(p).wait()
        return carry
    lax.fori_loop(1, wide, end_rows, 0)

    def place_copy(p):
        return pltpu.make_async_copy(
            row_land.at[p], row_scalar.at[(me + wide - p) % wide], row_recv.at[p]
        )

    def begin_place(p, carry):
        place_copy(p).start()
        return carry
    lax.fori_loop(1, wide, begin_place, 0)

    def end_place(p, carry):
        place_copy(p).wait()
        return carry
    lax.fori_loop(1, wide, end_place, 0)

    def y_copy(q):
        return pltpu.make_async_remote_copy(
            src_ref=partial.at[q, 1 - y_me], dst_ref=first_land.at[q], send_sem=y_send.at[q], recv_sem=y_recv.at[q],
            device_id={"wide": me + 2 - 4 * y_me}, device_id_type=MESH,
        )

    def z_copy(q, p):
        to = (z_me + p) % z_count
        return pltpu.make_async_remote_copy(
            src_ref=first.at[q, to], dst_ref=second_land.at[q, p],
            send_sem=z_send.at[q, p], recv_sem=z_recv.at[q, p],
            device_id={"wide": to * 4 + me % 4}, device_id_type=MESH,
        )

    def x_copy(q):
        return pltpu.make_async_remote_copy(
            src_ref=second.at[q, 1 - x_me], dst_ref=third_land.at[q], send_sem=x_send.at[q], recv_sem=x_recv.at[q],
            device_id={"wide": me + 1 - 2 * x_me}, device_id_type=MESH,
        )

    group = 8
    for q in range(chunks):
        for side in range(2):
            halo_copy(q, side).wait()

            def widen(i, carry):
                rows = pl.ds(pl.multiple_of(i * order, order), order)
                wide_halo[side, rows, :] = jnp.concatenate(split_bf16(halo[q, side, rows, :]), axis=1)
                return carry
            lax.fori_loop(0, REACH, widen, 0)
        for b in range(slab_rows):
            side = 0 if b < half_rows else 1
            low_h, high_h = (b, REACH) if side == 0 else (0, b + REACH - slab_rows + 1)
            if low_h >= high_h:
                continue
            got = dot(band[b, :, low_h * order:high_h * order], wide_halo[side, low_h * order:high_h * order, :])
            mixed[q, b * order:(b + 1) * order, :] += got[:order, :LANES] + (got[:order, LANES:] + got[order:, :LANES])

        def pick(w, carry):
            sign = parity_sign(w & me, (wide - 1).bit_length())
            for i in range(0, per_slab, group):
                found = [mixed[q, pl.ds(within(row_scalar[w, 0, i + k], slab_total), 1), :] for k in range(group)]
                partial[q, w // 2 % 2, w // 4, w % 2, i:i + group, :] = jnp.concatenate(found, axis=0) * sign
            return carry
        lax.fori_loop(0, wide, pick, 0)
        y_copy(q).start()
        y_copy(q).wait()
        first[q] = partial[q, y_me] + first_land[q]

        def begin_z(p, carry):
            z_copy(q, p).start()
            return carry
        lax.fori_loop(1, z_count, begin_z, 0)
        second[q] = first[q, z_me]

        def end_z(p, carry):
            z_copy(q, p).wait()
            second[q] += second_land[q, p]
            return carry
        lax.fori_loop(1, z_count, end_z, 0)
        x_copy(q).start()
        x_copy(q).wait()
        out[:, q * LANES:(q + 1) * LANES] = (second[q, x_me] + third_land[q]) * scale


def local(blocks, vectors, sign_bits, column_blocks, sample_rows):
    slab_rows, slots, order = blocks.shape[:3]
    wide = lax.axis_size("wide")
    shares = lax.axis_size("narrow")
    width = vectors.shape[1] // shares
    chunks = width // LANES
    slab_total = slab_rows * order
    per_slab = sample_rows.shape[0]
    z_count = wide // 4
    scale = math.sqrt(slab_total / per_slab) / math.sqrt(order * wide)
    hbm = pl.BlockSpec(memory_space=pl.ANY)
    vmem = pl.BlockSpec(memory_space=pltpu.VMEM)
    f32, bf16, i32 = jnp.float32, jnp.bfloat16, jnp.int32
    dma = pltpu.SemaphoreType.DMA
    return pl.pallas_call(
        functools.partial(sketch_kernel, scale),
        in_specs=[hbm, hbm, vmem, vmem, vmem],
        out_specs=vmem,
        out_shape=jax.ShapeDtypeStruct((per_slab, width), f32),
        scratch_shapes=[
            pltpu.VMEM((shares, slab_rows, slots, order, order), f32),
            pltpu.VMEM((slab_total, width), f32),
            pltpu.VMEM((slab_rows + 1, order, width), bf16),
            pltpu.VMEM((slab_rows + 1, order, width), bf16),
            pltpu.VMEM((chunks, 2, REACH * order, LANES), f32),
            pltpu.VMEM((2, REACH * order, 2 * LANES), bf16),
            pltpu.VMEM((order, REACH * order), f32),
            pltpu.VMEM((slab_rows, 2 * order, REACH * order), bf16),
            pltpu.VMEM((chunks, slab_total, LANES), f32),
            pltpu.VMEM((shares, slab_rows, slots), i32),
            pltpu.SMEM((shares, slab_rows, slots), i32),
            pltpu.VMEM((wide, 1, per_slab), i32),
            pltpu.SMEM((wide, 1, per_slab), i32),
            pltpu.VMEM((chunks, 2, z_count, 2, per_slab, LANES), f32),
            pltpu.VMEM((chunks, z_count, 2, per_slab, LANES), f32),
            pltpu.VMEM((chunks, z_count, 2, per_slab, LANES), f32),
            pltpu.VMEM((chunks, 2, per_slab, LANES), f32),
            pltpu.VMEM((chunks, z_count, 2, per_slab, LANES), f32),
            pltpu.VMEM((chunks, per_slab, LANES), f32),
            dma((slab_rows + 3,)),
            dma((shares, slab_rows)),
            dma((shares, slab_rows)),
            dma((chunks, 2)),
            dma((chunks, 2)),
            dma((shares,)),
            dma((shares,)),
            dma((wide,)),
            dma((wide,)),
            dma((chunks,)),
            dma((chunks,)),
            dma((chunks, z_count)),
            dma((chunks, z_count)),
            dma((chunks,)),
            dma((chunks,)),
        ],
        compiler_params=pltpu.CompilerParams(
            has_side_effects=True, collective_id=0, vmem_limit_bytes=60 << 20
        ),
        name="sketch",
    )(blocks, vectors, sign_bits.reshape(slab_rows, 1, order), column_blocks, sample_rows.reshape(1, per_slab))


def solution(mesh):
    return jax.shard_map(
        local,
        mesh=mesh,
        in_specs=(
            P("wide", "narrow", None, None),
            P("wide", None),
            P("wide"),
            P("wide", "narrow"),
            P("wide"),
        ),
        out_specs=P("wide", "narrow"),
        check_vma=False,
    )
```

time: 106 us -> 89.7 us (0.85)
  Pallas kernels: 65 us -> 85.8 us
  waiting for transfers between devices: 16.4 us -> 0 us
  starting transfers between devices: 14.9 us -> 0 us
  other arithmetic: 3.8 us -> 0 us
  local copies, waits for them, and re-layouts: 5.47 us -> 2.83 us
    pallas_call x3 -> x1, Pallas kernels: 65 us -> 85.8 us  [local(): pl.pallas_call(functools.partial(sketch_kernel, scale), in_specs=[hbm, hb...]
    ppermute x10 -> x0, waiting for transfers between devices: 16.4 us -> none  [the longest x1 12.9 us: local(): before = lax.ppermute(last_rows, 'wide', up)]
    ppermute x10 -> x0, starting transfers between devices: 14.9 us -> none  [the longest x6 8.52 us: widen(): parts.append(lax.ppermute(gathered, 'wide', pairs))]
    dynamic_slice x1 -> x0, local copies, waits for them, and re-layouts: 1.68 us -> none  [local(): lax.dynamic_slice(vectors, (0, narrow_me * half), (reach_rows, half))]
    select_n x5 -> x0, other arithmetic: 1.39 us -> none  [the longest x1 0.7 us: local(): local_columns = (column_blocks - me * slab_rows + REACH) % total_blocks]
    unnamed x7 -> x2, local copies, waits for them, and re-layouts: 1.48 us -> 2.83 us
    reduce_sum x2 -> x0, local copies, waits for them, and re-layouts: 1.35 us -> none  [the longest x1 0.68 us: local(): columns = jnp.sum(chosen * columns[:, None, :], axis=2)]
    convert_element_type x4 -> x0, other arithmetic: 1.25 us -> none  [the longest x2 1.24 us: parity_sign(): return (1 - 2 * (lax.population_count(bits) & 1)).astype(jnp.float32)]
  transfers between devices with their start and end apart: 10 -> 0, of which waited for: 3 -> 0; matrix products, arithmetic and copies ran while one was open for 7% -> 0% of each run, Pallas kernels for 17% -> 0%
where the time goes in v1:
time: 89.7 us; the launch traced here: 88.6 us
  Pallas kernels  85.8 us (96%)
  local copies, waits for them, and re-layouts  2.83 us (3%)
    pallas_call x1, Pallas kernels, local(): pl.pallas_call(functools.partial(sketch_kernel, scale), in_specs=[hbm, hb...  85.8 us
    unnamed x2, local copies, waits for them, and re-layouts  2.83 us

profile of v1, /device:TPU:0, one launch (start us, length us, event | category | flops | bytes accessed | tf_op | source)
XLA Modules:
  0.0 88.6 jit_solution(17429481220895495623)
XLA Ops:
  0.0 1.4 %copy.6.columns = s32[16,7]{1,0:T(8,128)} copy(s32[16,7]{0,1:T(8,128)} %param.8) | data formatting | bytes 896 | tf_op args[3]
  1.4 85.8 %sketch.1 = f32[64,256]{1,0:T(8,128)} custom-call(f32[16,7,128,128]{3,2,1,0:T(8,128)} %blocks.1, f32[2048,512]{1,0:T(8,128)} %vectors.1, s32[16,1,128]{2,1,0:T(1,128)} %bitcast.2, s32[16,7]{1,0:T(8,128)} %copy.6.columns, s32[1,64]{1,0:T(1,128)} %bitcast.3), custom_call_target="tpu_custom_call" | custom-call | tf_op jit(solution)/shard_map/sketch/pallas_call | solution.py:300
  87.2 1.5 %copy.8 = f32[64,256]{1,0:T(8,128)} copy(f32[64,256]{1,0:T(8,128)} %sketch.1) | data formatting | bytes 131072

commit v2 on v1

--- a/solution.py
+++ b/solution.py
@@ -38,8 +38,10 @@
     scale, blocks, vectors, signs, columns, samples, out,
     held_blocks, own, high, low, halo, wide_halo, outside, band, mixed, column_land, column_scalar, row_land,
     row_scalar, partial, first, first_land, second, second_land, third_land,
+    last_partial, near_land, total, far_land,
     local_sem, block_send, block_recv, halo_send, halo_recv, column_send, column_recv, row_send, row_recv,
     y_send, y_recv, z_send, z_recv, x_send, x_recv,
+    near_send, near_recv, far_send, far_recv,
 ):
     wide = lax.axis_size("wide")
     shares = lax.axis_size("narrow")
@@ -52,7 +54,7 @@
     per_slab = out.shape[0]
     reach_rows = REACH * order
     half_rows = slab_rows // 2
-    x_me, y_me, z_me = me % 2, me // 2 % 2, me // 4
+    x_me, y_me, z_me, near_me = me % 2, me // 2 % 2, me // 4, me % 4
     z_count = wide // 4
 
     barrier = pltpu.get_barrier_semaphore()
@@ -121,9 +123,8 @@
         row_copy(p).start()
         return carry
     lax.fori_loop(1, wide, begin_rows, 0)
-    for q in range(chunks):
-        for side in range(2):
-            halo_copy(q, side).start()
+    for side in range(2):
+        halo_copy(0, side).start()
 
     def begin_shares(b, carry):
         for p in range(1, shares):
@@ -152,6 +153,7 @@
     at_row = lax.broadcasted_iota(jnp.int32, (order, order), 0)
     at_column = lax.broadcasted_iota(jnp.int32, (order, order), 1)
     hadamard = parity_sign(at_row & at_column, (order - 1).bit_length())
+    release_row = slab_rows - 3
     entries = [(p, j) for p in range(shares) for j in range(slots)]
 
     def row(b, carry):
@@ -160,7 +162,7 @@
             share_copy(p, b).wait()
         place = []
         for p, j in entries:
-            at = column_scalar[p, b, j] - me * slab_rows + REACH
+            at = column_scalar[p, j, b] - me * slab_rows + REACH
             at = jnp.where(at < 0, at + total_blocks, at)
             place.append(jnp.where(at >= total_blocks, at - total_blocks, at))
         left, left_high, right_high, right_low = [], [], [], []
@@ -193,6 +195,14 @@
         t_high, t_low = split_bf16(turned)
         band[b, :order] = t_high
         band[b, order:] = t_low
+
+        @pl.when(b == release_row)
+        def _():
+            for side in range(2):
+                halo_copy(0, side).wait_send()
+            for q in range(1, chunks):
+                for side in range(2):
+                    halo_copy(q, side).start()
         return carry
     lax.fori_loop(0, slab_rows, row, 0)
 
@@ -238,10 +248,37 @@
             device_id={"wide": me + 1 - 2 * x_me}, device_id_type=MESH,
         )
 
+    def near_copy(p):
+        to = (near_me + p) % 4
+        return pltpu.make_async_remote_copy(
+            src_ref=last_partial.at[to], dst_ref=near_land.at[p],
+            send_sem=near_send.at[p], recv_sem=near_recv.at[p],
+            device_id={"wide": z_me * 4 + to}, device_id_type=MESH,
+        )
+
+    def far_copy(p):
+        to = (z_me + p) % z_count
+        return pltpu.make_async_remote_copy(
+            src_ref=total.at[to], dst_ref=far_land.at[p],
+            send_sem=far_send.at[p], recv_sem=far_recv.at[p],
+            device_id={"wide": to * 4 + near_me}, device_id_type=MESH,
+        )
+
     group = 8
+
+    def pick(q, w, to):
+        sign = parity_sign(w & me, (wide - 1).bit_length())
+        for i in range(0, per_slab, group):
+            found = [mixed[q, pl.ds(within(row_scalar[w, 0, i + k], slab_total), 1), :] for k in range(group)]
+            to[i:i + group, :] = jnp.concatenate(found, axis=0) * sign
+
+    last = chunks - 1
     for q in range(chunks):
         for side in range(2):
-            halo_copy(q, side).wait()
+            if q == 0:
+                halo_copy(q, side).wait_recv()
+            else:
+                halo_copy(q, side).wait()
 
             def widen(i, carry):
                 rows = pl.ds(pl.multiple_of(i * order, order), order)
@@ -256,21 +293,38 @@
             got = dot(band[b, :, low_h * order:high_h * order], wide_halo[side, low_h * order:high_h * order, :])
             mixed[q, b * order:(b + 1) * order, :] += got[:order, :LANES] + (got[:order, LANES:] + got[order:, :LANES])
 
-        def pick(w, carry):
-            sign = parity_sign(w & me, (wide - 1).bit_length())
-            for i in range(0, per_slab, group):
-                found = [mixed[q, pl.ds(within(row_scalar[w, 0, i + k], slab_total), 1), :] for k in range(group)]
-                partial[q, w // 2 % 2, w // 4, w % 2, i:i + group, :] = jnp.concatenate(found, axis=0) * sign
-            return carry
-        lax.fori_loop(0, wide, pick, 0)
-        y_copy(q).start()
-        y_copy(q).wait()
-        first[q] = partial[q, y_me] + first_land[q]
-
-        def begin_z(p, carry):
-            z_copy(q, p).start()
-            return carry
-        lax.fori_loop(1, z_count, begin_z, 0)
+        if q < last:
+            def pick_one(w, carry):
+                pick(q, w, partial.at[q, w // 2 % 2, w // 4, w % 2])
+                return carry
+            lax.fori_loop(0, wide, pick_one, 0)
+            y_copy(q).start()
+            y_copy(q).wait()
+            first[q] = partial[q, y_me] + first_land[q]
+
+            def begin_z(p, carry):
+                z_copy(q, p).start()
+                return carry
+            lax.fori_loop(1, z_count, begin_z, 0)
+        else:
+            def pick_near(p, carry):
+                to = (near_me + p) % 4
+
+                def pick_far(z, carry):
+                    pick(q, z * 4 + to, last_partial.at[to, z])
+                    return carry
+                lax.fori_loop(0, z_count, pick_far, 0)
+
+                return carry
+
+            def send_near(p, carry):
+                pick_near(p, carry)
+                near_copy(p).start()
+                return carry
+            lax.fori_loop(1, 4, send_near, 0)
+            pick_near(0, 0)
+
+    for q in range(last):
         second[q] = first[q, z_me]
 
         def end_z(p, carry):
@@ -279,8 +333,27 @@
             return carry
         lax.fori_loop(1, z_count, end_z, 0)
         x_copy(q).start()
+    total[...] = last_partial[near_me]
+
+    def end_near(p, carry):
+        near_copy(p).wait()
+        total[...] += near_land[p]
+        return carry
+    lax.fori_loop(1, 4, end_near, 0)
+
+    def begin_far(p, carry):
+        far_copy(p).start()
+        return carry
+    lax.fori_loop(1, z_count, begin_far, 0)
+    for q in range(last):
         x_copy(q).wait()
         out[:, q * LANES:(q + 1) * LANES] = (second[q, x_me] + third_land[q]) * scale
+    final = total[z_me]
+
+    def end_far(p, final):
+        far_copy(p).wait()
+        return final + far_land[p]
+    out[:, last * LANES:] = lax.fori_loop(1, z_count, end_far, final) * scale
 
 
 def local(blocks, vectors, sign_bits, column_blocks, sample_rows):
@@ -289,6 +362,7 @@
     shares = lax.axis_size("narrow")
     width = vectors.shape[1] // shares
     chunks = width // LANES
+    early = max(chunks - 1, 1)
     slab_total = slab_rows * order
     per_slab = sample_rows.shape[0]
     z_count = wide // 4
@@ -312,16 +386,20 @@
             pltpu.VMEM((order, REACH * order), f32),
             pltpu.VMEM((slab_rows, 2 * order, REACH * order), bf16),
             pltpu.VMEM((chunks, slab_total, LANES), f32),
-            pltpu.VMEM((shares, slab_rows, slots), i32),
-            pltpu.SMEM((shares, slab_rows, slots), i32),
+            pltpu.VMEM((shares, slots, slab_rows), i32),
+            pltpu.SMEM((shares, slots, slab_rows), i32),
             pltpu.VMEM((wide, 1, per_slab), i32),
             pltpu.SMEM((wide, 1, per_slab), i32),
-            pltpu.VMEM((chunks, 2, z_count, 2, per_slab, LANES), f32),
-            pltpu.VMEM((chunks, z_count, 2, per_slab, LANES), f32),
-            pltpu.VMEM((chunks, z_count, 2, per_slab, LANES), f32),
-            pltpu.VMEM((chunks, 2, per_slab, LANES), f32),
-            pltpu.VMEM((chunks, z_count, 2, per_slab, LANES), f32),
-            pltpu.VMEM((chunks, per_slab, LANES), f32),
+            pltpu.VMEM((early, 2, z_count, 2, per_slab, LANES), f32),
+            pltpu.VMEM((early, z_count, 2, per_slab, LANES), f32),
+            pltpu.VMEM((early, z_count, 2, per_slab, LANES), f32),
+            pltpu.VMEM((early, 2, per_slab, LANES), f32),
+            pltpu.VMEM((early, z_count, 2, per_slab, LANES), f32),
+            pltpu.VMEM((early, per_slab, LANES), f32),
+            pltpu.VMEM((4, z_count, per_slab, LANES), f32),
+            pltpu.VMEM((4, z_count, per_slab, LANES), f32),
+            pltpu.VMEM((z_count, per_slab, LANES), f32),
+            pltpu.VMEM((z_count, per_slab, LANES), f32),
             dma((slab_rows + 3,)),
             dma((shares, slab_rows)),
             dma((shares, slab_rows)),
@@ -337,12 +415,16 @@
             dma((chunks, z_count)),
             dma((chunks,)),
             dma((chunks,)),
+            dma((4,)),
+            dma((4,)),
+            dma((z_count,)),
+            dma((z_count,)),
         ],
         compiler_params=pltpu.CompilerParams(
             has_side_effects=True, collective_id=0, vmem_limit_bytes=60 << 20
         ),
         name="sketch",
-    )(blocks, vectors, sign_bits.reshape(slab_rows, 1, order), column_blocks, sample_rows.reshape(1, per_slab))
+    )(blocks, vectors, sign_bits.reshape(slab_rows, 1, order), column_blocks.T, sample_rows.reshape(1, per_slab))
 
 
 def solution(mesh):

time: 89.7 us -> 71.2 us (0.79)
  Pallas kernels: 85.8 us -> 69.5 us
  local copies, waits for them, and re-layouts: 2.83 us -> 1.47 us
    pallas_call x1, Pallas kernels: 85.8 us -> 69.5 us  [local(): pl.pallas_call(functools.partial(sketch_kernel, scale), in_specs=[hbm, hb...]
    unnamed x2 -> x1, local copies, waits for them, and re-layouts: 2.83 us -> 1.47 us
where the time goes in v2:
time: 71.2 us; the launch traced here: 71 us
  Pallas kernels  69.5 us (98%)
  local copies, waits for them, and re-layouts  1.47 us (2%)
    pallas_call x1, Pallas kernels, local(): pl.pallas_call(functools.partial(sketch_kernel, scale), in_specs=[hbm, hb...  69.5 us
    unnamed x1, local copies, waits for them, and re-layouts  1.47 us

profile of v2, /device:TPU:0, one launch (start us, length us, event | category | flops | bytes accessed | tf_op | source)
XLA Modules:
  0.0 71.0 jit_solution(13513838375030616340)
XLA Ops:
  0.0 69.5 %sketch.1 = f32[64,256]{1,0:T(8,128)} custom-call(f32[16,7,128,128]{3,2,1,0:T(8,128)} %blocks.1, f32[2048,512]{1,0:T(8,128)} %vectors.1, s32[16,1,128]{2,1,0:T(1,128)} %bitcast.3, s32[7,16]{1,0:T(8,128)} %bitcast.4, s32[1,64]{1,0:T(1,128)} %bitcast.5), custom_call_target="tpu_custom_call" | custom-call | tf_op jit(solution)/shard_map/sketch/pallas_call | solution.py:374
  69.5 1.5 %copy.7 = f32[64,256]{1,0:T(8,128)} copy(f32[64,256]{1,0:T(8,128)} %sketch.1) | data formatting | bytes 131072

commit v3 on v2

--- a/solution.py
+++ b/solution.py
@@ -9,6 +9,8 @@
 from jax.sharding import PartitionSpec as P
 
 REACH = 8
+FAR = 3
+NEAR = REACH - FAR
 LANES = 128
 MESH = pl.DeviceIdType.MESH
 
@@ -18,12 +20,16 @@
     return high, (x - high.astype(jnp.float32)).astype(jnp.bfloat16)
 
 
-def parity_sign(bits, width):
+def parity(bits, width):
     shift = 1 << max(width - 1, 1).bit_length() >> 1
     while shift:
         bits = bits ^ (bits >> shift)
         shift //= 2
-    return (1 - 2 * (bits & 1)).astype(jnp.float32)
+    return bits & 1
+
+
+def parity_sign(bits, width):
+    return (1 - 2 * parity(bits, width)).astype(jnp.float32)
 
 
 def within(value, count):
@@ -36,12 +42,14 @@
 
 def sketch_kernel(
     scale, blocks, vectors, signs, columns, samples, out,
-    held_blocks, own, high, low, halo, wide_halo, outside, band, mixed, column_land, column_scalar, row_land,
+    held_blocks, own, high, low, halo, wide_halo, outside, outside_far, band, mixed, both_mixed, column_land, column_scalar, row_land,
     row_scalar, partial, first, first_land, second, second_land, third_land,
     last_partial, near_land, total, far_land,
+    edge, edge_land, edge_band, edge_product,
     local_sem, block_send, block_recv, halo_send, halo_recv, column_send, column_recv, row_send, row_recv,
     y_send, y_recv, z_send, z_recv, x_send, x_recv,
     near_send, near_recv, far_send, far_recv,
+    edge_send, edge_recv, pass_send, pass_recv,
 ):
     wide = lax.axis_size("wide")
     shares = lax.axis_size("narrow")
@@ -52,7 +60,7 @@
     width = out.shape[1]
     chunks = width // LANES
     per_slab = out.shape[0]
-    reach_rows = REACH * order
+    near_rows = NEAR * order
     half_rows = slab_rows // 2
     x_me, y_me, z_me, near_me = me % 2, me // 2 % 2, me // 4, me % 4
     z_count = wide // 4
@@ -108,12 +116,32 @@
         )
 
     def halo_copy(q, side):
-        start = slab_total - reach_rows if side == 0 else 0
+        start = slab_total - near_rows if side == 0 else 0
         to = (me + 1) % wide if side == 0 else (me + wide - 1) % wide
         return pltpu.make_async_remote_copy(
-            src_ref=vectors.at[pl.ds(start, reach_rows), pl.ds(pl.multiple_of(part * width + q * LANES, LANES), LANES)],
+            src_ref=vectors.at[pl.ds(start, near_rows), pl.ds(pl.multiple_of(part * width + q * LANES, LANES), LANES)],
             dst_ref=halo.at[q, side], send_sem=halo_send.at[q, side], recv_sem=halo_recv.at[q, side],
             device_id={"wide": to}, device_id_type=MESH,
+        )
+
+    def edge_span(side, i):
+        return pl.ds(i * order, (FAR - i) * order) if side == 0 else pl.ds(0, (i + 1) * order)
+
+    def edge_copy(side, i):
+        to = (me + wide - 1) % wide if side == 0 else (me + 1) % wide
+        span = edge_span(side, i)
+        return pltpu.make_async_remote_copy(
+            src_ref=edge.at[side, i, :, span], dst_ref=edge_land.at[side, i, :, span],
+            send_sem=edge_send.at[side, i], recv_sem=edge_recv.at[side, i],
+            device_id={"wide": to}, device_id_type=MESH,
+        )
+
+    def pass_copy(side, i, p):
+        span = edge_span(side, i)
+        return pltpu.make_async_remote_copy(
+            src_ref=edge_land.at[side, i, :, span], dst_ref=edge_land.at[side, i, :, span],
+            send_sem=pass_send.at[side, i, p], recv_sem=pass_recv.at[side, i, p],
+            device_id=partner(p), device_id_type=MESH,
         )
 
     for p in range(1, shares):
@@ -126,9 +154,13 @@
     for side in range(2):
         halo_copy(0, side).start()
 
-    def begin_shares(b, carry):
+    def row_at(r):
+        last_rows = slab_rows - FAR + r - FAR
+        return jnp.where(r < FAR, r, jnp.where(r < 2 * FAR, last_rows, r - FAR))
+
+    def begin_shares(r, carry):
         for p in range(1, shares):
-            share_copy(p, b).start()
+            share_copy(p, row_at(r)).start()
         return carry
     lax.fori_loop(0, slab_rows, begin_shares, 0)
 
@@ -156,7 +188,8 @@
     release_row = slab_rows - 3
     entries = [(p, j) for p in range(shares) for j in range(slots)]
 
-    def row(b, carry):
+    def row(r, carry):
+        b = row_at(r)
         block_copy(b).wait()
         for p in range(1, shares):
             share_copy(p, b).wait()
@@ -178,12 +211,17 @@
         small = dot(jnp.concatenate(left_high, axis=1), jnp.concatenate(right_low, axis=0))
         product = both[:order] + (both[order:] + small)
 
-        first_out = jnp.where(b < half_rows, 0, REACH + slab_rows)
-        for h in range(REACH):
+        def gather(target):
             piece = jnp.zeros((order, order), jnp.float32)
             for (p, j), at in zip(entries, place):
-                piece = piece + held_blocks[p, b, j] * (at - first_out == h).astype(jnp.float32)
-            outside[:, h * order:(h + 1) * order] = piece
+                piece = piece + held_blocks[p, b, j] * (at == target).astype(jnp.float32)
+            return piece
+
+        first_near = jnp.where(b < half_rows, FAR, REACH + slab_rows)
+        for k in range(NEAR):
+            @pl.when(jnp.where(b < half_rows, FAR + k >= b, k <= b + REACH - slab_rows))
+            def _():
+                outside[:, k * order:(k + 1) * order] = gather(first_near + k)
 
         sign = (2 * signs[b] - 1).astype(jnp.float32)
         mix = (hadamard * sign).astype(jnp.bfloat16)
@@ -196,7 +234,28 @@
         band[b, :order] = t_high
         band[b, order:] = t_low
 
-        @pl.when(b == release_row)
+        @pl.when(r < 2 * FAR)
+        def _():
+            side_at = jnp.where(r < FAR, 0, 1)
+            first_far = jnp.where(r < FAR, 0, REACH + slab_rows + NEAR)
+            for k in range(FAR):
+                outside_far[:, k * order:(k + 1) * order] = gather(first_far + k)
+            edge[side_at, r - FAR * side_at] = dot(mix, jnp.concatenate(split_bf16(outside_far[...]), axis=0))
+
+        for side in range(2):
+            @pl.when((r == (side + 1) * FAR) & (part == side % shares))
+            def _():
+                for i in range(FAR):
+                    edge_copy(side, i).start()
+
+            @pl.when((r == slab_rows - 2) & (part == side % shares))
+            def _():
+                for i in range(FAR):
+                    edge_copy(side, i).wait()
+                    for p in range(1, shares):
+                        pass_copy(side, i, p).start()
+
+        @pl.when(r == release_row)
         def _():
             for side in range(2):
                 halo_copy(0, side).wait_send()
@@ -264,13 +323,46 @@
             device_id={"wide": to * 4 + near_me}, device_id_type=MESH,
         )
 
+    for side in range(2):
+        for i in range(FAR):
+            for p in range(1, shares):
+                @pl.when(part == side % shares)
+                def _():
+                    pass_copy(side, i, p).wait_send()
+
+                @pl.when((part + p) % shares == side % shares)
+                def _():
+                    pass_copy(side, i, shares - p).wait_recv()
+            steps = range(i, FAR) if side == 0 else range(i + 1)
+            first_block = slab_rows - REACH if side == 0 else NEAR
+            span = slice(steps[0] * order, (steps[-1] + 1) * order)
+            edge_high, edge_low = split_bf16(edge_land[side, i, :, span])
+            edge_band[side, i, :order, span] = edge_high
+            edge_band[side, i, order:, span] = edge_low
+            both = dot(
+                edge_band[side, i, :, span], jnp.concatenate([high[first_block + k] for k in steps], axis=0)
+            )
+            small = dot(
+                edge_band[side, i, :order, span], jnp.concatenate([low[first_block + k] for k in steps], axis=0)
+            )
+            edge_product[side, i] = both[:order] + (both[order:] + small)
+
     group = 8
-
-    def pick(q, w, to):
-        sign = parity_sign(w & me, (wide - 1).bit_length())
+    index_bits = (wide - 1).bit_length()
+
+    def flipped(w, slab):
+        return parity(w & (me ^ slab), index_bits)
+
+    def pick(w, to):
+        sign = parity_sign(w & me, index_bits)
+        upper = flipped(w, (me + 1) % wide) * slab_total
+        lower = flipped(w, (me + wide - 1) % wide) * slab_total
+
+        def found(i):
+            at = within(row_scalar[w, 0, i], slab_total)
+            return both_mixed[pl.ds(at + jnp.where(at < half_rows * order, upper, lower), 1), :]
         for i in range(0, per_slab, group):
-            found = [mixed[q, pl.ds(within(row_scalar[w, 0, i + k], slab_total), 1), :] for k in range(group)]
-            to[i:i + group, :] = jnp.concatenate(found, axis=0) * sign
+            to[i:i + group, :] = jnp.concatenate([found(i + k) for k in range(group)], axis=0) * sign
 
     last = chunks - 1
     for q in range(chunks):
@@ -284,34 +376,47 @@
                 rows = pl.ds(pl.multiple_of(i * order, order), order)
                 wide_halo[side, rows, :] = jnp.concatenate(split_bf16(halo[q, side, rows, :]), axis=1)
                 return carry
-            lax.fori_loop(0, REACH, widen, 0)
+            lax.fori_loop(0, NEAR, widen, 0)
         for b in range(slab_rows):
-            side = 0 if b < half_rows else 1
-            low_h, high_h = (b, REACH) if side == 0 else (0, b + REACH - slab_rows + 1)
-            if low_h >= high_h:
-                continue
-            got = dot(band[b, :, low_h * order:high_h * order], wide_halo[side, low_h * order:high_h * order, :])
-            mixed[q, b * order:(b + 1) * order, :] += got[:order, :LANES] + (got[:order, LANES:] + got[order:, :LANES])
-
+            at = slice(b * order, (b + 1) * order)
+            value = mixed[q, at, :]
+            if b < half_rows:
+                side, begin, end, edge_at = 0, max(b, FAR), REACH, b
+            else:
+                side, begin, end, edge_at = 1, 0, min(b + REACH - slab_rows + 1, NEAR), b + FAR - slab_rows
+            if begin < end:
+                shift = FAR if side == 0 else 0
+                got = dot(
+                    band[b, :, (begin - shift) * order:(end - shift) * order],
+                    wide_halo[side, (begin - shift) * order:(end - shift) * order, :],
+                )
+                value = value + (got[:order, :LANES] + (got[:order, LANES:] + got[order:, :LANES]))
+            change = 0
+            if 0 <= edge_at < FAR:
+                change = edge_product[side, edge_at, :, q * LANES:(q + 1) * LANES]
+            both_mixed[at, :] = value + change
+            both_mixed[slab_total + b * order:slab_total + (b + 1) * order, :] = value - change
+
+        if q > 0:
+            y_copy(q - 1).wait()
+            first[q - 1] = partial[q - 1, y_me] + first_land[q - 1]
+
+            def begin_z(p, carry):
+                z_copy(q - 1, p).start()
+                return carry
+            lax.fori_loop(1, z_count, begin_z, 0)
         if q < last:
             def pick_one(w, carry):
-                pick(q, w, partial.at[q, w // 2 % 2, w // 4, w % 2])
+                pick(w, partial.at[q, w // 2 % 2, w // 4, w % 2])
                 return carry
             lax.fori_loop(0, wide, pick_one, 0)
             y_copy(q).start()
-            y_copy(q).wait()
-            first[q] = partial[q, y_me] + first_land[q]
-
-            def begin_z(p, carry):
-                z_copy(q, p).start()
-                return carry
-            lax.fori_loop(1, z_count, begin_z, 0)
         else:
             def pick_near(p, carry):
                 to = (near_me + p) % 4
 
                 def pick_far(z, carry):
-                    pick(q, z * 4 + to, last_partial.at[to, z])
+                    pick(z * 4 + to, last_partial.at[to, z])
                     return carry
                 lax.fori_loop(0, z_count, pick_far, 0)
 
@@ -381,11 +486,13 @@
             pltpu.VMEM((slab_total, width), f32),
             pltpu.VMEM((slab_rows + 1, order, width), bf16),
             pltpu.VMEM((slab_rows + 1, order, width), bf16),
-            pltpu.VMEM((chunks, 2, REACH * order, LANES), f32),
-            pltpu.VMEM((2, REACH * order, 2 * LANES), bf16),
-            pltpu.VMEM((order, REACH * order), f32),
-            pltpu.VMEM((slab_rows, 2 * order, REACH * order), bf16),
+            pltpu.VMEM((chunks, 2, NEAR * order, LANES), f32),
+            pltpu.VMEM((2, NEAR * order, 2 * LANES), bf16),
+            pltpu.VMEM((order, NEAR * order), f32),
+            pltpu.VMEM((order, FAR * order), f32),
+            pltpu.VMEM((slab_rows, 2 * order, NEAR * order), bf16),
             pltpu.VMEM((chunks, slab_total, LANES), f32),
+            pltpu.VMEM((2 * slab_total, LANES), f32),
             pltpu.VMEM((shares, slots, slab_rows), i32),
             pltpu.SMEM((shares, slots, slab_rows), i32),
             pltpu.VMEM((wide, 1, per_slab), i32),
@@ -400,6 +507,10 @@
             pltpu.VMEM((4, z_count, per_slab, LANES), f32),
             pltpu.VMEM((z_count, per_slab, LANES), f32),
             pltpu.VMEM((z_count, per_slab, LANES), f32),
+            pltpu.VMEM((2, FAR, order, FAR * order), f32),
+            pltpu.VMEM((2, FAR, order, FAR * order), f32),
+            pltpu.VMEM((2, FAR, 2 * order, FAR * order), bf16),
+            pltpu.VMEM((2, FAR, order, width), f32),
             dma((slab_rows + 3,)),
             dma((shares, slab_rows)),
             dma((shares, slab_rows)),
@@ -419,6 +530,10 @@
             dma((4,)),
             dma((z_count,)),
             dma((z_count,)),
+            dma((2, FAR)),
+            dma((2, FAR)),
+            dma((2, FAR, shares)),
+            dma((2, FAR, shares)),
         ],
         compiler_params=pltpu.CompilerParams(
             has_side_effects=True, collective_id=0, vmem_limit_bytes=60 << 20

time: 71.2 us -> 67.8 us (0.952)
  Pallas kernels: 69.5 us -> 66.1 us
    pallas_call x1, Pallas kernels: 69.5 us -> 66.1 us  [local(): pl.pallas_call(functools.partial(sketch_kernel, scale), in_specs=[hbm, hb...]
where the time goes in v3:
time: 67.8 us; the launch traced here: 67.6 us
  Pallas kernels  66.1 us (97%)
  local copies, waits for them, and re-layouts  1.47 us (2%)
    pallas_call x1, Pallas kernels, local(): pl.pallas_call(functools.partial(sketch_kernel, scale), in_specs=[hbm, hb...  66.1 us
    unnamed x1, local copies, waits for them, and re-layouts  1.47 us

profile of v3, /device:TPU:0, one launch (start us, length us, event | category | flops | bytes accessed | tf_op | source)
XLA Modules:
  0.0 67.6 jit_solution(1915792310639216732)
XLA Ops:
  0.0 66.1 %sketch.1 = f32[64,256]{1,0:T(8,128)} custom-call(f32[16,7,128,128]{3,2,1,0:T(8,128)} %blocks.1, f32[2048,512]{1,0:T(8,128)} %vectors.1, s32[16,1,128]{2,1,0:T(1,128)} %bitcast.3, s32[7,16]{1,0:T(8,128)} %bitcast.4, s32[1,64]{1,0:T(1,128)} %bitcast.5), custom_call_target="tpu_custom_call" | custom-call | tf_op jit(solution)/shard_map/sketch/pallas_call | solution.py:479
  66.1 1.5 %copy.7 = f32[64,256]{1,0:T(8,128)} copy(f32[64,256]{1,0:T(8,128)} %sketch.1) | data formatting | bytes 131072

commit v4 on v3

--- a/solution.py
+++ b/solution.py
@@ -9,7 +9,7 @@
 from jax.sharding import PartitionSpec as P
 
 REACH = 8
-FAR = 3
+FAR = 2
 NEAR = REACH - FAR
 LANES = 128
 MESH = pl.DeviceIdType.MESH

time: 67.8 us -> 67.1 us (0.990)
  Pallas kernels: 66.1 us -> 65.4 us
    pallas_call x1, Pallas kernels: 66.1 us -> 65.4 us  [local(): pl.pallas_call(functools.partial(sketch_kernel, scale), in_specs=[hbm, hb...]
where the time goes in v4:
time: 67.1 us; the launch traced here: 66.9 us
  Pallas kernels  65.4 us (97%)
  local copies, waits for them, and re-layouts  1.47 us (2%)
    pallas_call x1, Pallas kernels, local(): pl.pallas_call(functools.partial(sketch_kernel, scale), in_specs=[hbm, hb...  65.4 us
    unnamed x1, local copies, waits for them, and re-layouts  1.47 us

profile of v4, /device:TPU:0, one launch (start us, length us, event | category | flops | bytes accessed | tf_op | source)
XLA Modules:
  0.0 66.9 jit_solution(11315254164033463861)
XLA Ops:
  0.0 65.4 %sketch.1 = f32[64,256]{1,0:T(8,128)} custom-call(f32[16,7,128,128]{3,2,1,0:T(8,128)} %blocks.1, f32[2048,512]{1,0:T(8,128)} %vectors.1, s32[16,1,128]{2,1,0:T(1,128)} %bitcast.3, s32[7,16]{1,0:T(8,128)} %bitcast.4, s32[1,64]{1,0:T(1,128)} %bitcast.5), custom_call_target="tpu_custom_call" | custom-call | tf_op jit(solution)/shard_map/sketch/pallas_call | solution.py:479
  65.4 1.5 %copy.7 = f32[64,256]{1,0:T(8,128)} copy(f32[64,256]{1,0:T(8,128)} %sketch.1) | data formatting | bytes 131072

commit v5 on v4

--- a/solution.py
+++ b/solution.py
@@ -397,14 +397,6 @@
             both_mixed[at, :] = value + change
             both_mixed[slab_total + b * order:slab_total + (b + 1) * order, :] = value - change
 
-        if q > 0:
-            y_copy(q - 1).wait()
-            first[q - 1] = partial[q - 1, y_me] + first_land[q - 1]
-
-            def begin_z(p, carry):
-                z_copy(q - 1, p).start()
-                return carry
-            lax.fori_loop(1, z_count, begin_z, 0)
         if q < last:
             def pick_one(w, carry):
                 pick(w, partial.at[q, w // 2 % 2, w // 4, w % 2])
@@ -427,6 +419,14 @@
                 near_copy(p).start()
                 return carry
             lax.fori_loop(1, 4, send_near, 0)
+            for e in range(last):
+                y_copy(e).wait()
+                first[e] = partial[e, y_me] + first_land[e]
+
+                def begin_z(p, carry):
+                    z_copy(e, p).start()
+                    return carry
+                lax.fori_loop(1, z_count, begin_z, 0)
             pick_near(0, 0)
 
     for q in range(last):

time: 67.1 us -> 65.6 us (0.978)
  Pallas kernels: 65.4 us -> 63.9 us
    pallas_call x1, Pallas kernels: 65.4 us -> 63.9 us  [local(): pl.pallas_call(functools.partial(sketch_kernel, scale), in_specs=[hbm, hb...]
where the time goes in v5:
time: 65.6 us; the launch traced here: 65.4 us
  Pallas kernels  63.9 us (97%)
  local copies, waits for them, and re-layouts  1.47 us (2%)
    pallas_call x1, Pallas kernels, local(): pl.pallas_call(functools.partial(sketch_kernel, scale), in_specs=[hbm, hb...  63.9 us
    unnamed x1, local copies, waits for them, and re-layouts  1.47 us

profile of v5, /device:TPU:0, one launch (start us, length us, event | category | flops | bytes accessed | tf_op | source)
XLA Modules:
  0.0 65.4 jit_solution(17271117342595091117)
XLA Ops:
  0.0 63.9 %sketch.1 = f32[64,256]{1,0:T(8,128)} custom-call(f32[16,7,128,128]{3,2,1,0:T(8,128)} %blocks.1, f32[2048,512]{1,0:T(8,128)} %vectors.1, s32[16,1,128]{2,1,0:T(1,128)} %bitcast.3, s32[7,16]{1,0:T(8,128)} %bitcast.4, s32[1,64]{1,0:T(1,128)} %bitcast.5), custom_call_target="tpu_custom_call" | custom-call | tf_op jit(solution)/shard_map/sketch/pallas_call | solution.py:479
  63.9 1.5 %copy.7 = f32[64,256]{1,0:T(8,128)} copy(f32[64,256]{1,0:T(8,128)} %sketch.1) | data formatting | bytes 131072
